TPU v7x, 256 devices: a whole 4x4x8 slice. The times are simulated.
256 devices in a mesh: row: 16 (over x, y_hi, core), col: 8 (over z), depth: 2 (over y_lo).
Axes of the slice: x: 4, y: 4 (y_hi: 2, y_lo: 2; y = y_hi * 2 + y_lo), z: 8, core: 2. Of those that a mesh axis runs over, the one named last changes fastest.
Arguments:
- front_matrix: float32 [2, 8192, 8192], P('depth', 'row', 'col'), as said below
- block_mask: int32 [2, 64, 64], P('depth', 'row', 'col'), may hold values 0 or 1
- supernode_width: int32 [2, 3], P('depth'), may hold values from 128 to 256, as said below
Outputs:
- schur: float32 [2, 8192, 8192], P('depth', 'row', 'col')
- ancestor: float32 [4096, 4096], P('row', ('col', 'depth'))
Inputs may be any that keep to these rules, and one draw needn't show every extreme that they name: `front_matrix`: restricted to its first 768 rows and columns, each front is row diagonally dominant: each diagonal entry is positive and at least 1.5 times the sum of the magnitudes of the other entries of its row among those columns. `supernode_width`: each entry is a multiple of 128; in each front one supernode has the full width 256.
All inputs are finite; a program needn't handle non-finite values. No bound on the sum of `block_mask` on one device may be relied on, other than what follows from the above.
Results may differ from a plain program's by a relative error of at most 0.0001.
Values sent between devices are 32-bit elements; how exact they have to be, the bound alone decides.
No kernel may reach another device: no remote copies, remote signals or barrier semaphores. Data moves between devices by JAX's collectives and lax.ppermute only.
A program may use at most 64 MiB of HBM per device.

v0:
```python
import jax
import jax.numpy as jnp
from jax import lax
from jax.experimental import pallas as pl
from jax.experimental.pallas import tpu as pltpu
from jax.sharding import PartitionSpec as P


SN = 256
BLK = 128
NSN = 3
PIV = SN * NSN
ROWS = 16
COLS = 8
CHIPS = 8
XS = 4


def split(a):
    high = a.astype(jnp.bfloat16)
    low = (a - high.astype(jnp.float32)).astype(jnp.bfloat16)
    return high, low


def mul(a, b):
    return jnp.dot(a, b, preferred_element_type=jnp.float32)


def stack(a):
    return jnp.concatenate(split(a), axis=0)


def dot3(a, b):
    rows = a.shape[0] // 2
    both = mul(a, b[0])
    return both[:rows] + (both[rows:] + mul(a[:rows], b[1]))


def inverse(block):
    shape = block.shape
    eye = lax.broadcasted_iota(jnp.int32, shape, 0) == lax.broadcasted_iota(jnp.int32, shape, 1)
    diagonal = jnp.where(eye, block, 0.0)
    by_row = 1.0 / jnp.sum(diagonal, axis=1, keepdims=True)
    by_col = 1.0 / jnp.sum(diagonal, axis=0, keepdims=True)
    power = jnp.where(eye, 0.0, -block * by_row)
    total = jnp.where(eye, 1.0, power)
    for _ in range(5):
        parts = split(power)
        power = dot3(jnp.concatenate(parts, axis=0), parts)
        total = total + dot3(stack(total), split(power))
    return total * by_col


def place_rows(target, own, other, info, columns=slice(None)):
    x, core = info[0], info[1]
    for parts, c in ((own, core), (other, 1 - core)):
        for k in range(XS):
            for e in range(2):
                chip = 2 * lax.rem(x + k, XS) + e
                target[pl.ds(pl.multiple_of(512 * c + 32 * chip, 32), 32), :] = parts[k][48 * e:48 * e + 32, columns]
                target[pl.ds(pl.multiple_of(256 + 128 * c + 16 * chip, 16), 16), :] = parts[k][48 * e + 32:48 * e + 48, columns]


def pieces_kernel(info, front, kept, moved, *out):
    first = info[1] == 0
    for q in range(CHIPS):
        out[q][:32, :] = front[32 * q:32 * q + 32, :] * kept[q // 4:q // 4 + 1, :]
        mine = front[256 + 16 * q:272 + 16 * q, :] * kept[2:3, :]
        out[q][32:, :] = jnp.where(first, mine, moved[16 * q:16 * q + 16, :])


def with_ones(info, value, i):
    row_ids = lax.broadcasted_iota(jnp.int32, (SN, SN), 0)
    col_ids = lax.broadcasted_iota(jnp.int32, (SN, SN), 1)
    return jnp.where((row_ids == col_ids) & (row_ids >= info[4 + i]), 1.0, value)


def put_pair(target, pair):
    target[:SN] = pair[0]
    target[SN:] = pair[1]


def factor_kernel(info, *refs):
    lower, upper, matrix = refs[8:]
    place_rows(matrix, refs[:4], refs[4:8], info)
    row_ids = lax.broadcasted_iota(jnp.int32, (SN, SN), 0)
    col_ids = lax.broadcasted_iota(jnp.int32, (SN, SN), 1)

    def block(i, j):
        keep = (row_ids < info[4 + i]) & (col_ids < info[4 + j])
        return jnp.where(keep, matrix[SN * i:SN * i + SN, SN * j:SN * j + SN], 0.0)

    i0 = inverse(with_ones(info, block(0, 0), 0))
    i0_parts, i0 = split(i0), stack(i0)
    v01 = dot3(i0, split(block(0, 1)))
    v02 = dot3(i0, split(block(0, 2)))
    v01_parts, v02_parts = split(v01), split(v02)
    m10 = stack(block(1, 0))
    m20 = stack(block(2, 0))
    i1 = inverse(with_ones(info, block(1, 1) - dot3(m10, v01_parts), 1))
    i1_parts, i1 = split(i1), stack(i1)
    m21 = stack(block(2, 1) - dot3(m20, v01_parts))
    v12 = split(dot3(i1, split(block(1, 2) - dot3(m10, v02_parts))))
    i2 = stack(inverse(with_ones(info, block(2, 2) - dot3(m20, v02_parts) - dot3(m21, v12), 2)))
    g10 = -dot3(i1, split(dot3(m10, i0_parts)))
    h20 = split(dot3(m20, i0_parts) + dot3(m21, split(g10)))
    h21 = split(dot3(m21, i1_parts))
    lower[0] = i0
    lower[1] = stack(g10)
    lower[2] = i1
    lower[3] = stack(-dot3(i2, h20))
    lower[4] = stack(-dot3(i2, h21))
    lower[5] = i2
    put_pair(upper.at[0], v01_parts)
    put_pair(upper.at[1], v12)
    put_pair(upper.at[2], split(v02 - dot3(stack(v01), v12)))


def order_of(info, offset, axis, shape):
    ids = offset + lax.broadcasted_iota(jnp.int32, shape, axis)
    order = jnp.full(shape, NSN, jnp.int32)
    for s in range(NSN):
        order = jnp.where((ids >= SN * s) & (ids < SN * s + info[4 + s]), s, order)
    return order


def left_of(info, panel, upper, left):
    def pair(n):
        return upper[n, :SN], upper[n, SN:]

    keep = lax.broadcasted_iota(jnp.int32, (512, SN), 1)
    order = order_of(info, info[3] * 512, 0, (512, 1))
    c = [jnp.where(keep < info[4 + s], panel[:, SN * s:SN * s + SN], 0.0) for s in range(NSN)]
    c0, c1 = stack(c[0]), stack(c[1])
    l1 = stack(c[1] - dot3(c0, pair(0)))
    l2 = stack(c[2] - dot3(c0, pair(2)) - dot3(c1, pair(1)))
    live = jnp.concatenate([order, order], axis=0)
    for s, value in enumerate((c0, l1, l2)):
        left[:, SN * s:SN * s + SN] = jnp.where(live > s, value, jnp.zeros_like(value))


def update_kernel(info, front, kept, *refs, again):
    own, other, lower = refs[:4], refs[4:8], refs[8]
    if again:
        left, _, out, quarter, band, block, sems = refs[9:]
    else:
        upper, panel, out, quarter, left, band, block, sems = refs[9:]
        left_of(info, panel, upper, left)
    half = info[8] if again else info[7]
    width = band.shape[1]
    columns = pl.ds(pl.multiple_of(half * 512, 512), 512)
    place_rows(band, own, other, info, columns)
    keep = lax.broadcasted_iota(jnp.int32, (SN, width), 0)
    r = [split(jnp.where(keep < info[4 + s], band[SN * s:SN * s + SN, :], 0.0)) for s in range(NSN)]
    s0 = split(dot3(lower[0], r[0]))
    s1 = split(dot3(lower[1], r[0]) + dot3(lower[2], r[1]))
    s2 = split(dot3(lower[3], r[0]) + dot3(lower[4], r[1]) + dot3(lower[5], r[2]))
    order = order_of(info, info[2] * 1024 + half * 512, 1, (1, width))
    total = None
    for s, value in enumerate((s0, s1, s2)):
        live = order > s
        masked = tuple(jnp.where(live, part, jnp.zeros_like(part)) for part in value)
        term = dot3(left[:, SN * s:SN * s + SN], masked)
        total = term if total is None else total + term
    copies = []
    for i in range(4):
        rows = slice(128 * i, 128 * i + 128)
        result = front[rows, columns] * kept[i:i + 1, columns] - total[rows]
        block[rows, :] = result
        copies.append(pltpu.make_async_copy(block.at[rows, :], out.at[rows, columns], sems.at[i]))
        copies[i].start()
        if i % 2:
            for j in range(2):
                quarter[64 * (i - 1):64 * (i + 1), 128 * j:128 * j + 128] = result[:, 256 * j + 128:256 * j + 256]
    for copy in copies:
        copy.wait()


VMEM_WHOLE = pl.BlockSpec(memory_space=pltpu.VMEM)


def each(axis_size, target):
    return [(i, target(i)) for i in range(axis_size)]


X_UP = each(ROWS, lambda i: (i + 4) % ROWS)
X_DOWN = each(ROWS, lambda i: (i - 4) % ROWS)
MATE = each(ROWS, lambda i: i ^ 2)
CORE = each(ROWS, lambda i: i ^ 1)
Z_ODD = [(z, z + 1) for z in range(0, COLS, 2)]


def gather_plane(piece, odd):
    height = piece.shape[0]
    mate = lax.ppermute(piece, "row", MATE)
    pair = jnp.concatenate([jnp.where(odd, mate, piece), jnp.where(odd, piece, mate)])
    before = lax.ppermute(pair, "row", X_UP)
    after = lax.ppermute(pair, "row", X_DOWN)
    far_even = lax.ppermute(before[:height], "row", X_UP)
    far_odd = lax.ppermute(after[height:], "row", X_DOWN)
    own = [pair, after, jnp.concatenate([far_even, far_odd]), before]
    return own, [lax.ppermute(part, "row", CORE) for part in own]


def exchange(front, kept, info, row_index, col_index):
    odd = (row_index // 2) % 2 == 1
    odd_col = col_index % 2 == 1
    moved = lax.ppermute(front[384:512] * kept[3:4], "row", [(0, 1)])
    pieces = pl.pallas_call(
        pieces_kernel,
        grid_spec=pltpu.PrefetchScalarGridSpec(
            num_scalar_prefetch=1,
            grid=(),
            in_specs=[VMEM_WHOLE] * 3,
            out_specs=[VMEM_WHOLE] * CHIPS,
        ),
        out_shape=[jax.ShapeDtypeStruct((48, 1024), jnp.float32)] * CHIPS,
        name="pieces",
    )(info, front, kept, moved)
    parts = [lax.ppermute(pieces[q], "row", [(0, 2 * q), (1, 2 * q + 1)]) for q in range(1, CHIPS)]
    piece = jnp.where(row_index < 2, pieces[0], sum(parts[1:], parts[0]))

    core_piece = piece[:, :PIV]
    parts = [lax.ppermute(core_piece, "col", [(0, z)]) for z in (2, 4, 6)]
    pivot_piece = jnp.where(col_index == 0, core_piece, parts[0] + parts[1] + parts[2])
    pivot_piece = jnp.where(odd_col, lax.ppermute(pivot_piece, "col", Z_ODD), pivot_piece)

    strips = [front[64 * z:64 * z + 64, :PIV] * kept[z // 2:z // 2 + 1, :PIV] for z in range(COLS)]
    parts = [lax.ppermute(strips[z], "col", [(0, z)]) for z in range(1, COLS)]
    strip = jnp.where(col_index == 0, strips[0], sum(parts[1:], parts[0]))
    panel = lax.all_to_all(jnp.broadcast_to(strip[None], (COLS, 64, PIV)), "col", 0, 0).reshape(512, PIV)

    return gather_plane(piece, odd), gather_plane(pivot_piece, odd), panel


def compute(info, front, kept, band, pivot, panel):
    stacked = lambda *n: jax.ShapeDtypeStruct((*n, 2 * SN, SN), jnp.bfloat16)
    lower, upper = pl.pallas_call(
        factor_kernel,
        grid_spec=pltpu.PrefetchScalarGridSpec(
            num_scalar_prefetch=1,
            grid=(),
            in_specs=[VMEM_WHOLE] * 8,
            out_specs=[VMEM_WHOLE] * 2,
            scratch_shapes=[pltpu.VMEM((PIV, PIV), jnp.float32)],
        ),
        out_shape=[stacked(6), stacked(3)],
        name="factor",
    )(info, *pivot[0], *pivot[1])

    def update(which, *inputs):
        left_shape = (1024, PIV)
        anywhere = pl.BlockSpec(memory_space=pl.ANY)
        specs = [VMEM_WHOLE, anywhere] if which else [VMEM_WHOLE] * len(inputs)
        return pl.pallas_call(
            lambda *refs: update_kernel(*refs, again=which == 1),
            grid_spec=pltpu.PrefetchScalarGridSpec(
                num_scalar_prefetch=1,
                grid=(),
                in_specs=[VMEM_WHOLE] * 11 + specs,
                out_specs=[anywhere, VMEM_WHOLE] + [VMEM_WHOLE] * (1 - which),
                scratch_shapes=[
                    pltpu.VMEM((PIV, 512), jnp.float32),
                    pltpu.VMEM((512, 512), jnp.float32),
                    pltpu.SemaphoreType.DMA((4,)),
                ],
            ),
            out_shape=[
                jax.ShapeDtypeStruct((512, 1024), jnp.float32),
                jax.ShapeDtypeStruct((256, 256), jnp.float32),
            ] + [jax.ShapeDtypeStruct(left_shape, jnp.bfloat16)] * (1 - which),
            input_output_aliases={13: 0} if which else {},
            name="update",
        )(info, front, kept, *band[0], *band[1], lower, *inputs)

    partial, leaving, left = update(0, upper, panel)
    arriving = lax.ppermute(leaving, "depth", [(0, 1), (1, 0)])
    result, staying = update(1, left, partial)
    return result[None], staying + arriving


def local(front_matrix, block_mask, supernode_width):
    row_index = lax.axis_index("row")
    col_index = lax.axis_index("col")
    depth_index = lax.axis_index("depth")
    block_rows = row_index * 4 + jnp.arange(4)
    block_cols = col_index * 8 + jnp.arange(8)
    kept = ((block_mask[0] != 0) | (block_rows[:, None] == block_cols[None, :])).astype(jnp.float32)
    kept = jnp.broadcast_to(kept[:, :, None], (4, 8, BLK)).reshape(4, 1024)
    front = front_matrix[0]
    info = jnp.concatenate([
        jnp.stack([row_index // 4, row_index % 2, col_index, row_index]).astype(jnp.int32),
        supernode_width[0],
        jnp.stack([1 - depth_index, depth_index]).astype(jnp.int32),
    ])
    panels = exchange(front, kept, info, row_index, col_index)
    return compute(info, front, kept, *panels)


def solution(mesh):
    placed = (P("depth", "row", "col"), P("depth", "row", "col"), P("depth", None))
    return jax.shard_map(
        local,
        mesh=mesh,
        in_specs=placed,
        out_specs=(P("depth", "row", "col"), P("row", ("col", "depth"))),
        check_vma=False,
    )
```

profile of v0, /device:TPU:1, one launch (start us, length us, event | category | flops | bytes accessed | tf_op | source)
XLA Modules:
  0.0 158.4 jit_solution(6057296136264968241)
XLA Ops:
  4.1 1.5 slice_multiply_fusion.5
  5.6 5.7 %collective-permute-start.31 = (f32[64,768]{1,0:T(8,128)S(1)}, f32[64,768]{1,0:T(8,128)S(1)}, u32[]{:S(2)}, u32[]{:S(2)}) collective-permute-start(f32[64,768]{1,0:T(8,128)S(1)} %get-tuple-element.38), channel_id=1, source_target_pairs={{0,4},{1,5},{16,20},{17,21},{32,36},{33,37},{48,52},{49,53},{64,68... | collective-permute-start | bytes 589832 | tf_op jit(solution)/shard_map/ppermute | solution.py:229
  11.4 2.0 %collective-permute-start.32 = (f32[64,768]{1,0:T(8,128)S(1)}, f32[64,768]{1,0:T(8,128)S(1)}, u32[]{:S(2)}, u32[]{:S(2)}) collective-permute-start(f32[64,768]{1,0:T(8,128)S(1)} %get-tuple-element.39), channel_id=1, source_target_pairs={{0,6},{1,7},{16,22},{17,23},{32,38},{33,39},{48,54},{49,55},{64,70... | collective-permute-start | bytes 589832 | tf_op jit(solution)/shard_map/ppermute | solution.py:229
  13.4 1.9 %collective-permute-start.36 = (f32[64,768]{1,0:T(8,128)S(1)}, f32[64,768]{1,0:T(8,128)S(1)}, u32[]{:S(2)}, u32[]{:S(2)}) collective-permute-start(f32[64,768]{1,0:T(8,128)S(1)} %get-tuple-element.44), channel_id=1, source_target_pairs={{0,14},{1,15},{16,30},{17,31},{32,46},{33,47},{48,62},{49,63},{64,... | collective-permute-start | bytes 589832 | tf_op jit(solution)/shard_map/ppermute | solution.py:229
  15.3 1.3 collective-permute-start.35
  18.7 3.5 %pieces.1 = (f32[48,1024]{1,0:T(8,128)}, f32[48,1024]{1,0:T(8,128)}, f32[48,1024]{1,0:T(8,128)}, f32[48,1024]{1,0:T(8,128)}, f32[48,1024]{1,0:T(8,128)}, /*index...) custom-call(s32[9]{0:T(128)} %concatenate.15.info.refs_0_, f32[512,1024]{1,0:T(8,128)} %bitcast.28, ...), custom_call_target="tpu_custom_call" | custom-call | tf_op jit(solution)/shard_map/pieces/pallas_call | solution.py:209
  23.5 1.3 collective-permute-start.30
  24.8 4.2 %collective-permute-start.1 = (f32[48,1024]{1,0:T(8,128)}, f32[48,1024]{1,0:T(8,128)S(1)}, u32[]{:S(2)}, u32[]{:S(2)}) collective-permute-start(f32[48,1024]{1,0:T(8,128)} %get-tuple-element.18), channel_id=1, source_target_pairs={{0,32},{16,48},{1,33},{17,49},{2,34},{18,50},{3,35},{19,51},{4,36}... | collective-permute-start | bytes 589832 | tf_op jit(solution)/shard_map/ppermute | solution.py:220
  29.1 1.3 collective-permute-start.2
  30.4 2.0 %collective-permute-start.3 = (f32[48,1024]{1,0:T(8,128)}, f32[48,1024]{1,0:T(8,128)S(1)}, u32[]{:S(2)}, u32[]{:S(2)}) collective-permute-start(f32[48,1024]{1,0:T(8,128)} %get-tuple-element.20), channel_id=1, source_target_pairs={{0,96},{16,112},{1,97},{17,113},{2,98},{18,114},{3,99},{19,115},{4... | collective-permute-start | bytes 589832 | tf_op jit(solution)/shard_map/ppermute | solution.py:220
  32.5 1.3 collective-permute-start.4
  33.8 4.2 %collective-permute-start.5 = (f32[48,1024]{1,0:T(8,128)}, f32[48,1024]{1,0:T(8,128)S(1)}, u32[]{:S(2)}, u32[]{:S(2)}) collective-permute-start(f32[48,1024]{1,0:T(8,128)} %get-tuple-element.22), channel_id=1, source_target_pairs={{0,160},{16,176},{1,161},{17,177},{2,162},{18,178},{3,163},{19,179... | collective-permute-start | bytes 589832 | tf_op jit(solution)/shard_map/ppermute | solution.py:220
  39.3 1.3 collective-permute-start.7
  42.9 3.9 %all-to-all-start = ((f32[8,64,768]{2,1,0:T(8,128)}), f32[8,64,768]{2,1,0:T(8,128)S(1)}, u32[]{:S(2)}, u32[]{:S(2)}) async-start(f32[8,64,768]{2,1,0:T(8,128)} %broadcast_in_dim.24), calls=%async_computation | async-start | bytes 3145728 | tf_op jit(solution)/shard_map/all_to_all | solution.py:231
  47.0 5.5 %collective-permute-start.19 = (f32[48,768]{1,0:T(8,128)S(1)}, f32[48,768]{1,0:T(8,128)S(1)}, u32[]{:S(2)}, u32[]{:S(2)}) collective-permute-start(f32[48,768]{1,0:T(8,128)S(1)} %slice.97), channel_id=1, source_target_pairs={{0,12},{1,13},{16,28},{17,29},{32,44},{33,45},{48,60},{49,61},{64,... | collective-permute-start | bytes 442376 | tf_op jit(solution)/shard_map/ppermute | solution.py:224
  52.4 2.5 %collective-permute-start.18 = (f32[48,768]{1,0:T(8,128)S(1)}, f32[48,768]{1,0:T(8,128)S(1)}, u32[]{:S(2)}, u32[]{:S(2)}) collective-permute-start(f32[48,768]{1,0:T(8,128)S(1)} %slice.97), channel_id=1, source_target_pairs={{0,8},{1,9},{16,24},{17,25},{32,40},{33,41},{48,56},{49,57},{64,72... | collective-permute-start | bytes 442376 | tf_op jit(solution)/shard_map/ppermute | solution.py:224
  56.2 14.2 %collective-permute-done.19 = f32[48,768]{1,0:T(8,128)S(1)} collective-permute-done((f32[48,768]{1,0:T(8,128)S(1)}, f32[48,768]{1,0:T(8,128)S(1)}, u32[]{:S(2)}, u32[]{:S(2)}) %collective-permute-start.19) | collective-permute-done | bytes 147488 | tf_op jit(solution)/shard_map/ppermute | solution.py:224
  70.4 9.4 %collective-permute-done.18 = f32[48,768]{1,0:T(8,128)S(1)} collective-permute-done((f32[48,768]{1,0:T(8,128)S(1)}, f32[48,768]{1,0:T(8,128)S(1)}, u32[]{:S(2)}, u32[]{:S(2)}) %collective-permute-start.18) | collective-permute-done | bytes 147488 | tf_op jit(solution)/shard_map/ppermute | solution.py:224
  79.8 4.0 %collective-permute-done.17 = f32[48,768]{1,0:T(8,128)S(1)} collective-permute-done((f32[48,768]{1,0:T(8,128)S(1)}, f32[48,768]{1,0:T(8,128)S(1)}, u32[]{:S(2)}, u32[]{:S(2)}) %collective-permute-start.17) | collective-permute-done | bytes 147488 | tf_op jit(solution)/shard_map/ppermute | solution.py:224
  85.3 3.9 %collective-permute-done.20 = f32[48,768]{1,0:T(8,128)S(1)} collective-permute-done((f32[48,768]{1,0:T(8,128)S(1)}, f32[48,768]{1,0:T(8,128)S(1)}, u32[]{:S(2)}, u32[]{:S(2)}) %collective-permute-start.20) | collective-permute-done | bytes 147488 | tf_op jit(solution)/shard_map/ppermute | solution.py:226
  89.4 1.9 %collective-permute-done.8 = f32[48,1024]{1,0:T(8,128)S(1)} collective-permute-done((f32[48,1024]{1,0:T(8,128)S(1)}, f32[48,1024]{1,0:T(8,128)S(1)}, u32[]{:S(2)}, u32[]{:S(2)}) %collective-permute-start.8) | collective-permute-done | bytes 196640 | tf_op jit(solution)/shard_map/ppermute | solution.py:195
  91.5 2.7 %collective-permute-start.9 = (f32[96,1024]{1,0:T(8,128)S(1)}, f32[96,1024]{1,0:T(8,128)S(1)}, u32[]{:S(2)}, u32[]{:S(2)}) collective-permute-start(f32[96,1024]{1,0:T(8,128)S(1)} %pad_maximum_fusion.refs_3_), channel_id=1, source_target_pairs={{0,192},{16,208},{32,224},{48,240},{64,0},{80,16},{96,32},{112,48}... | collective-permute-start | bytes 1179656 | tf_op jit(solution)/shard_map/ppermute | solution.py:198
  95.0 2.7 %collective-permute-start.22 = (f32[96,768]{1,0:T(8,128)S(1)}, f32[96,768]{1,0:T(8,128)S(1)}, u32[]{:S(2)}, u32[]{:S(2)}) collective-permute-start(f32[96,768]{1,0:T(8,128)S(1)} %pad_maximum_fusion.1.refs_0_), channel_id=1, source_target_pairs={{0,192},{16,208},{32,224},{48,240},{64,0},{80,16},{96,32},{112,48}... | collective-permute-start | bytes 884744 | tf_op jit(solution)/shard_map/ppermute | solution.py:198
  97.7 1.9 %collective-permute-done.10.refs_6_ = f32[96,1024]{1,0:T(8,128)S(1)} collective-permute-done((f32[96,1024]{1,0:T(8,128)S(1)}, f32[96,1024]{1,0:T(8,128)S(1)}, u32[]{:S(2)}, u32[]{:S(2)}) %collective-permute-start.10) | collective-permute-done | bytes 393248 | tf_op jit(solution)/shard_map/ppermute | solution.py:197
  99.8 2.7 %collective-permute-start.12 = (f32[48,1024]{1,0:T(8,128)S(1)}, f32[48,1024]{1,0:T(8,128)S(1)}, u32[]{:S(2)}, u32[]{:S(2)}) collective-permute-start(f32[48,1024]{1,0:T(8,128)S(1)} %slice.96), channel_id=1, source_target_pairs={{0,192},{16,208},{32,224},{48,240},{64,0},{80,16},{96,32},{112,48}... | collective-permute-start | bytes 589832 | tf_op jit(solution)/shard_map/ppermute | solution.py:200
  102.5 10.4 %collective-permute-start.26 = (f32[96,768]{1,0:T(8,128)S(1)}, f32[96,768]{1,0:T(8,128)S(1)}, u32[]{:S(2)}, u32[]{:S(2)}) collective-permute-start(f32[96,768]{1,0:T(8,128)S(1)} %pad_maximum_fusion.1.refs_0_), channel_id=1, source_target_pairs={{0,16},{16,0},{32,48},{48,32},{64,80},{80,64},{96,112},{112,96},{1... | collective-permute-start | bytes 884744 | tf_op jit(solution)/shard_map/ppermute | solution.py:202
  113.1 2.7 %collective-permute-start.25 = (f32[48,768]{1,0:T(8,128)S(1)}, f32[48,768]{1,0:T(8,128)S(1)}, u32[]{:S(2)}, u32[]{:S(2)}) collective-permute-start(f32[48,768]{1,0:T(8,128)S(1)} %slice.99), channel_id=1, source_target_pairs={{0,192},{16,208},{32,224},{48,240},{64,0},{80,16},{96,32},{112,48}... | collective-permute-start | bytes 442376 | tf_op jit(solution)/shard_map/ppermute | solution.py:200
  116.6 3.0 %collective-permute-done.24 = f32[48,768]{1,0:T(8,128)S(1)} collective-permute-done((f32[48,768]{1,0:T(8,128)S(1)}, f32[48,768]{1,0:T(8,128)S(1)}, u32[]{:S(2)}, u32[]{:S(2)}) %collective-permute-start.24) | collective-permute-done | bytes 147488 | tf_op jit(solution)/shard_map/ppermute | solution.py:199
  124.1 12.5 %factor.1 = (bf16[6,512,256]{2,1,0:T(8,128)(2,1)}, bf16[3,512,256]{2,1,0:T(8,128)(2,1)}) custom-call(s32[9]{0:T(128)} %concatenate.15.info.refs_0_, f32[96,768]{1,0:T(8,128)} %copy-done.6, f32[96,768]{1,0:T(8,128)} %copy-done.8, f32[96,768]{1,0:T(8,128)} %copy-done.9, f32[96,768]{1,0:T(8,128)} %copy-done.7, f32[96,768]{1,0:T(8,128)} %copy-done.12, ...), custom_call_target="tpu_custom_call" | custom-call | tf_op jit(solution)/shard_map/factor/pallas_call | solution.py:238
  137.9 9.8 %update.2 = (f32[512,1024]{1,0:T(8,128)}, f32[256,256]{1,0:T(8,128)}, bf16[1024,768]{1,0:T(8,128)(2,1)}) custom-call(s32[9]{0:T(128)} %concatenate.15.info.refs_0_, f32[512,1024]{1,0:T(8,128)} %bitcast.30, f32[4,1024]{1,0:T(4,128)} %bitcast.36, f32[96,1024]{1,0:T(8,128)} %copy-done.1, f32[96,1024]{1,0:T(8,128)} %copy-done.3, f32[96,1024]{1,0:T(8,128)} %copy-done.4, ...), custom_call_target="tpu_custom_call" | custom-call | tf_op jit(solution)/shard_map/update/pallas_call | solution.py:255
  148.3 8.5 %update.3 = (f32[512,1024]{1,0:T(8,128)}, f32[256,256]{1,0:T(8,128)}) custom-call(s32[9]{0:T(128)} %concatenate.15.info.refs_0_, f32[512,1024]{1,0:T(8,128)} %bitcast.31, f32[4,1024]{1,0:T(4,128)} %bitcast.37, f32[96,1024]{1,0:T(8,128)} %copy-done.1, f32[96,1024]{1,0:T(8,128)} %copy-done.3, f32[96,1024]{1,0:T(8,128)} %copy-done.4, ...), custom_call_target="tpu_custom_call", output_to_operand_aliasing={{0}: (13, {})} | custom-call | tf_op jit(solution)/shard_map/update/pallas_call | solution.py:255
  156.8 1.7 %add.98 = f32[256,256]{1,0:T(8,128)} add(f32[256,256]{1,0:T(8,128)} %get-tuple-element.30, f32[256,256]{1,0:T(8,128)S(1)} %collective-permute-done.37) | non-fusion elementwise | flops 65536 | bytes 786432 | tf_op jit(solution)/shard_map/add | solution.py:279
  (115 shorter events, 21.4 us)
Async XLA Ops:
  2.6 14.7 %collective-permute-start = (f32[128,1024]{1,0:T(8,128)S(1)}, f32[128,1024]{1,0:T(8,128)S(1)}, u32[]{:S(2)}, u32[]{:S(2)}) collective-permute-start(f32[128,1024]{1,0:T(8,128)S(1)} %bitcast_multiply_fusion), channel_id=1, source_target_pairs={{0,16},{1,17},{2,18},{3,19},{4,20},{5,21},{6,22},{7,23},{8,24},{9,... | collective-permute-start | bytes 1572872 | tf_op jit(solution)/shard_map/ppermute | solution.py:208
  5.6 16.6 %collective-permute-start.31 = (f32[64,768]{1,0:T(8,128)S(1)}, f32[64,768]{1,0:T(8,128)S(1)}, u32[]{:S(2)}, u32[]{:S(2)}) collective-permute-start(f32[64,768]{1,0:T(8,128)S(1)} %get-tuple-element.38), channel_id=1, source_target_pairs={{0,4},{1,5},{16,20},{17,21},{32,36},{33,37},{48,52},{49,53},{64,68... | collective-permute-start | bytes 589832 | tf_op jit(solution)/shard_map/ppermute | solution.py:229
  11.4 12.1 %collective-permute-start.32 = (f32[64,768]{1,0:T(8,128)S(1)}, f32[64,768]{1,0:T(8,128)S(1)}, u32[]{:S(2)}, u32[]{:S(2)}) collective-permute-start(f32[64,768]{1,0:T(8,128)S(1)} %get-tuple-element.39), channel_id=1, source_target_pairs={{0,6},{1,7},{16,22},{17,23},{32,38},{33,39},{48,54},{49,55},{64,70... | collective-permute-start | bytes 589832 | tf_op jit(solution)/shard_map/ppermute | solution.py:229
  13.4 11.4 %collective-permute-start.36 = (f32[64,768]{1,0:T(8,128)S(1)}, f32[64,768]{1,0:T(8,128)S(1)}, u32[]{:S(2)}, u32[]{:S(2)}) collective-permute-start(f32[64,768]{1,0:T(8,128)S(1)} %get-tuple-element.44), channel_id=1, source_target_pairs={{0,14},{1,15},{16,30},{17,31},{32,46},{33,47},{48,62},{49,63},{64,... | collective-permute-start | bytes 589832 | tf_op jit(solution)/shard_map/ppermute | solution.py:229
  15.3 13.8 %collective-permute-start.35 = (f32[64,768]{1,0:T(8,128)S(1)}, f32[64,768]{1,0:T(8,128)S(1)}, u32[]{:S(2)}, u32[]{:S(2)}) collective-permute-start(f32[64,768]{1,0:T(8,128)S(1)} %get-tuple-element.45), channel_id=1, source_target_pairs={{0,12},{1,13},{16,28},{17,29},{32,44},{33,45},{48,60},{49,61},{64,... | collective-permute-start | bytes 589832 | tf_op jit(solution)/shard_map/ppermute | solution.py:229
  17.3 13.1 %collective-permute-start.34 = (f32[64,768]{1,0:T(8,128)S(1)}, f32[64,768]{1,0:T(8,128)S(1)}, u32[]{:S(2)}, u32[]{:S(2)}) collective-permute-start(f32[64,768]{1,0:T(8,128)S(1)} %get-tuple-element.46), channel_id=1, source_target_pairs={{0,10},{1,11},{16,26},{17,27},{32,42},{33,43},{48,58},{49,59},{64,... | collective-permute-start | bytes 589832 | tf_op jit(solution)/shard_map/ppermute | solution.py:229
  22.2 10.3 %collective-permute-start.33 = (f32[64,768]{1,0:T(8,128)S(1)}, f32[64,768]{1,0:T(8,128)S(1)}, u32[]{:S(2)}, u32[]{:S(2)}) collective-permute-start(f32[64,768]{1,0:T(8,128)S(1)} %get-tuple-element.47), channel_id=1, source_target_pairs={{0,8},{1,9},{16,24},{17,25},{32,40},{33,41},{48,56},{49,57},{64,72... | collective-permute-start | bytes 589832 | tf_op jit(solution)/shard_map/ppermute | solution.py:229
  23.5 10.3 %collective-permute-start.30 = (f32[64,768]{1,0:T(8,128)S(1)}, f32[64,768]{1,0:T(8,128)S(1)}, u32[]{:S(2)}, u32[]{:S(2)}) collective-permute-start(f32[64,768]{1,0:T(8,128)S(1)} %get-tuple-element.48), channel_id=1, source_target_pairs={{0,2},{1,3},{16,18},{17,19},{32,34},{33,35},{48,50},{49,51},{64,66... | collective-permute-start | bytes 589832 | tf_op jit(solution)/shard_map/ppermute | solution.py:229
  24.8 13.1 %collective-permute-start.1 = (f32[48,1024]{1,0:T(8,128)}, f32[48,1024]{1,0:T(8,128)S(1)}, u32[]{:S(2)}, u32[]{:S(2)}) collective-permute-start(f32[48,1024]{1,0:T(8,128)} %get-tuple-element.18), channel_id=1, source_target_pairs={{0,32},{16,48},{1,33},{17,49},{2,34},{18,50},{3,35},{19,51},{4,36}... | collective-permute-start | bytes 589832 | tf_op jit(solution)/shard_map/ppermute | solution.py:220
  29.1 10.2 %collective-permute-start.2 = (f32[48,1024]{1,0:T(8,128)}, f32[48,1024]{1,0:T(8,128)S(1)}, u32[]{:S(2)}, u32[]{:S(2)}) collective-permute-start(f32[48,1024]{1,0:T(8,128)} %get-tuple-element.19), channel_id=1, source_target_pairs={{0,64},{16,80},{1,65},{17,81},{2,66},{18,82},{3,67},{19,83},{4,68}... | collective-permute-start | bytes 589832 | tf_op jit(solution)/shard_map/ppermute | solution.py:220
  30.4 16.4 %collective-permute-start.3 = (f32[48,1024]{1,0:T(8,128)}, f32[48,1024]{1,0:T(8,128)S(1)}, u32[]{:S(2)}, u32[]{:S(2)}) collective-permute-start(f32[48,1024]{1,0:T(8,128)} %get-tuple-element.20), channel_id=1, source_target_pairs={{0,96},{16,112},{1,97},{17,113},{2,98},{18,114},{3,99},{19,115},{4... | collective-permute-start | bytes 589832 | tf_op jit(solution)/shard_map/ppermute | solution.py:220
  32.5 14.3 %collective-permute-start.4 = (f32[48,1024]{1,0:T(8,128)}, f32[48,1024]{1,0:T(8,128)S(1)}, u32[]{:S(2)}, u32[]{:S(2)}) collective-permute-start(f32[48,1024]{1,0:T(8,128)} %get-tuple-element.21), channel_id=1, source_target_pairs={{0,128},{16,144},{1,129},{17,145},{2,130},{18,146},{3,131},{19,147... | collective-permute-start | bytes 589832 | tf_op jit(solution)/shard_map/ppermute | solution.py:220
  33.8 13.0 %collective-permute-start.5 = (f32[48,1024]{1,0:T(8,128)}, f32[48,1024]{1,0:T(8,128)S(1)}, u32[]{:S(2)}, u32[]{:S(2)}) collective-permute-start(f32[48,1024]{1,0:T(8,128)} %get-tuple-element.22), channel_id=1, source_target_pairs={{0,160},{16,176},{1,161},{17,177},{2,162},{18,178},{3,163},{19,179... | collective-permute-start | bytes 589832 | tf_op jit(solution)/shard_map/ppermute | solution.py:220
  38.0 8.9 %collective-permute-start.6 = (f32[48,1024]{1,0:T(8,128)}, f32[48,1024]{1,0:T(8,128)S(1)}, u32[]{:S(2)}, u32[]{:S(2)}) collective-permute-start(f32[48,1024]{1,0:T(8,128)} %get-tuple-element.23), channel_id=1, source_target_pairs={{0,192},{16,208},{1,193},{17,209},{2,194},{18,210},{3,195},{19,211... | collective-permute-start | bytes 589832 | tf_op jit(solution)/shard_map/ppermute | solution.py:220
  39.3 7.5 %collective-permute-start.7 = (f32[48,1024]{1,0:T(8,128)}, f32[48,1024]{1,0:T(8,128)S(1)}, u32[]{:S(2)}, u32[]{:S(2)}) collective-permute-start(f32[48,1024]{1,0:T(8,128)} %get-tuple-element.24), channel_id=1, source_target_pairs={{0,224},{16,240},{1,225},{17,241},{2,226},{18,242},{3,227},{19,243... | collective-permute-start | bytes 589832 | tf_op jit(solution)/shard_map/ppermute | solution.py:220
  42.9 93.8 %all-to-all-start = ((f32[8,64,768]{2,1,0:T(8,128)}), f32[8,64,768]{2,1,0:T(8,128)S(1)}, u32[]{:S(2)}, u32[]{:S(2)}) async-start(f32[8,64,768]{2,1,0:T(8,128)} %broadcast_in_dim.24), calls=%async_computation | async-start | bytes 3145728 | tf_op jit(solution)/shard_map/all_to_all | solution.py:231
  47.0 23.5 %collective-permute-start.19 = (f32[48,768]{1,0:T(8,128)S(1)}, f32[48,768]{1,0:T(8,128)S(1)}, u32[]{:S(2)}, u32[]{:S(2)}) collective-permute-start(f32[48,768]{1,0:T(8,128)S(1)} %slice.97), channel_id=1, source_target_pairs={{0,12},{1,13},{16,28},{17,29},{32,44},{33,45},{48,60},{49,61},{64,... | collective-permute-start | bytes 442376 | tf_op jit(solution)/shard_map/ppermute | solution.py:224
  52.4 27.3 %collective-permute-start.18 = (f32[48,768]{1,0:T(8,128)S(1)}, f32[48,768]{1,0:T(8,128)S(1)}, u32[]{:S(2)}, u32[]{:S(2)}) collective-permute-start(f32[48,768]{1,0:T(8,128)S(1)} %slice.97), channel_id=1, source_target_pairs={{0,8},{1,9},{16,24},{17,25},{32,40},{33,41},{48,56},{49,57},{64,72... | collective-permute-start | bytes 442376 | tf_op jit(solution)/shard_map/ppermute | solution.py:224
  54.9 28.9 %collective-permute-start.17 = (f32[48,768]{1,0:T(8,128)S(1)}, f32[48,768]{1,0:T(8,128)S(1)}, u32[]{:S(2)}, u32[]{:S(2)}) collective-permute-start(f32[48,768]{1,0:T(8,128)S(1)} %slice.97), channel_id=1, source_target_pairs={{0,4},{1,5},{16,20},{17,21},{32,36},{33,37},{48,52},{49,53},{64,68... | collective-permute-start | bytes 442376 | tf_op jit(solution)/shard_map/ppermute | solution.py:224
  91.4 8.2 %collective-permute-start.10 = (f32[96,1024]{1,0:T(8,128)S(1)}, f32[96,1024]{1,0:T(8,128)S(1)}, u32[]{:S(2)}, u32[]{:S(2)}) collective-permute-start(f32[96,1024]{1,0:T(8,128)S(1)} %pad_maximum_fusion.refs_3_), channel_id=1, source_target_pairs={{0,64},{16,80},{32,96},{48,112},{64,128},{80,144},{96,160},{112,17... | collective-permute-start | bytes 1179656 | tf_op jit(solution)/shard_map/ppermute | solution.py:197
  91.5 8.2 %collective-permute-start.9 = (f32[96,1024]{1,0:T(8,128)S(1)}, f32[96,1024]{1,0:T(8,128)S(1)}, u32[]{:S(2)}, u32[]{:S(2)}) collective-permute-start(f32[96,1024]{1,0:T(8,128)S(1)} %pad_maximum_fusion.refs_3_), channel_id=1, source_target_pairs={{0,192},{16,208},{32,224},{48,240},{64,0},{80,16},{96,32},{112,48}... | collective-permute-start | bytes 1179656 | tf_op jit(solution)/shard_map/ppermute | solution.py:198
  94.9 18.0 %collective-permute-start.23 = (f32[96,768]{1,0:T(8,128)S(1)}, f32[96,768]{1,0:T(8,128)S(1)}, u32[]{:S(2)}, u32[]{:S(2)}) collective-permute-start(f32[96,768]{1,0:T(8,128)S(1)} %pad_maximum_fusion.1.refs_0_), channel_id=1, source_target_pairs={{0,64},{16,80},{32,96},{48,112},{64,128},{80,144},{96,160},{112,17... | collective-permute-start | bytes 884744 | tf_op jit(solution)/shard_map/ppermute | solution.py:197
  95.0 18.0 %collective-permute-start.22 = (f32[96,768]{1,0:T(8,128)S(1)}, f32[96,768]{1,0:T(8,128)S(1)}, u32[]{:S(2)}, u32[]{:S(2)}) collective-permute-start(f32[96,768]{1,0:T(8,128)S(1)} %pad_maximum_fusion.1.refs_0_), channel_id=1, source_target_pairs={{0,192},{16,208},{32,224},{48,240},{64,0},{80,16},{96,32},{112,48}... | collective-permute-start | bytes 884744 | tf_op jit(solution)/shard_map/ppermute | solution.py:198
  99.6 16.2 %collective-permute-start.11 = (f32[48,1024]{1,0:T(8,128)S(1)}, f32[48,1024]{1,0:T(8,128)S(1)}, u32[]{:S(2)}, u32[]{:S(2)}) collective-permute-start(f32[48,1024]{1,0:T(8,128)S(1)} %slice.95), channel_id=1, source_target_pairs={{0,64},{16,80},{32,96},{48,112},{64,128},{80,144},{96,160},{112,17... | collective-permute-start | bytes 589832 | tf_op jit(solution)/shard_map/ppermute | solution.py:199
  99.8 16.7 %collective-permute-start.12 = (f32[48,1024]{1,0:T(8,128)S(1)}, f32[48,1024]{1,0:T(8,128)S(1)}, u32[]{:S(2)}, u32[]{:S(2)}) collective-permute-start(f32[48,1024]{1,0:T(8,128)S(1)} %slice.96), channel_id=1, source_target_pairs={{0,192},{16,208},{32,224},{48,240},{64,0},{80,16},{96,32},{112,48}... | collective-permute-start | bytes 589832 | tf_op jit(solution)/shard_map/ppermute | solution.py:200
  102.5 18.0 %collective-permute-start.26 = (f32[96,768]{1,0:T(8,128)S(1)}, f32[96,768]{1,0:T(8,128)S(1)}, u32[]{:S(2)}, u32[]{:S(2)}) collective-permute-start(f32[96,768]{1,0:T(8,128)S(1)} %pad_maximum_fusion.1.refs_0_), channel_id=1, source_target_pairs={{0,16},{16,0},{32,48},{48,32},{64,80},{80,64},{96,112},{112,96},{1... | collective-permute-start | bytes 884744 | tf_op jit(solution)/shard_map/ppermute | solution.py:202
  113.1 7.6 %collective-permute-start.25 = (f32[48,768]{1,0:T(8,128)S(1)}, f32[48,768]{1,0:T(8,128)S(1)}, u32[]{:S(2)}, u32[]{:S(2)}) collective-permute-start(f32[48,768]{1,0:T(8,128)S(1)} %slice.99), channel_id=1, source_target_pairs={{0,192},{16,208},{32,224},{48,240},{64,0},{80,16},{96,32},{112,48}... | collective-permute-start | bytes 442376 | tf_op jit(solution)/shard_map/ppermute | solution.py:200
  119.6 17.0 %collective-permute-start.13 = (f32[96,1024]{1,0:T(8,128)S(1)}, f32[96,1024]{1,0:T(8,128)S(1)}, u32[]{:S(2)}, u32[]{:S(2)}) collective-permute-start(f32[96,1024]{1,0:T(8,128)S(1)} %pad_maximum_fusion.refs_3_), channel_id=1, source_target_pairs={{0,16},{16,0},{32,48},{48,32},{64,80},{80,64},{96,112},{112,96},{1... | collective-permute-start | bytes 1179656 | tf_op jit(solution)/shard_map/ppermute | solution.py:202
  120.5 16.1 %collective-permute-start.16 = (f32[96,1024]{1,0:T(8,128)S(1)}, f32[96,1024]{1,0:T(8,128)}, u32[]{:S(2)}, u32[]{:S(2)}) collective-permute-start(f32[96,1024]{1,0:T(8,128)S(1)} %collective-permute-done.10.refs_6_), channel_id=1, source_target_pairs={{0,16},{16,0},{32,48},{48,32},{64,80},{80,64},{96,112},{112,96},{1... | collective-permute-start | bytes 1179656 | tf_op jit(solution)/shard_map/ppermute | solution.py:202
  120.6 16.0 %collective-permute-start.14 = (f32[96,1024]{1,0:T(8,128)S(1)}, f32[96,1024]{1,0:T(8,128)}, u32[]{:S(2)}, u32[]{:S(2)}) collective-permute-start(f32[96,1024]{1,0:T(8,128)S(1)} %collective-permute-done.9.refs_4_), channel_id=1, source_target_pairs={{0,16},{16,0},{32,48},{48,32},{64,80},{80,64},{96,112},{112,96},{1... | collective-permute-start | bytes 1179656 | tf_op jit(solution)/shard_map/ppermute | solution.py:202
  121.1 15.5 %collective-permute-start.15 = (f32[96,1024]{1,0:T(8,128)S(1)}, f32[96,1024]{1,0:T(8,128)}, u32[]{:S(2)}, u32[]{:S(2)}) collective-permute-start(f32[96,1024]{1,0:T(8,128)S(1)} %constant_dynamic-update-slice_fusion.refs_5_), channel_id=1, source_target_pairs={{0,16},{16,0},{32,48},{48,32},{64,80},{80,64},{96,112},{112,96},{1... | collective-permute-start | bytes 1179656 | tf_op jit(solution)/shard_map/ppermute | solution.py:202
  147.8 9.0 %collective-permute-start.37 = (f32[256,256]{1,0:T(8,128)}, f32[256,256]{1,0:T(8,128)S(1)}, u32[]{:S(2)}, u32[]{:S(2)}) collective-permute-start(f32[256,256]{1,0:T(8,128)} %get-tuple-element.31), channel_id=1, source_target_pairs={{0,1},{1,0},{2,3},{3,2},{4,5},{5,4},{6,7},{7,6},{8,9},{9,8},{10,11... | collective-permute-start | bytes 786440 | tf_op jit(solution)/shard_map/ppermute | solution.py:277
  (24 other events, 261.8 us)
where the time goes:
time: 159 us; the launch traced here: 158 us
  starting transfers between devices  71.2 us (45%)
  waiting for transfers between devices  40.5 us (25%)
  Pallas kernels  34.3 us (22%)
  other arithmetic  6.4 us (4%)
  local copies, waits for them, and re-layouts  4.58 us (3%)
    ppermute x3, waiting for transfers between devices, exchange(): parts = [lax.ppermute(core_piece, 'col', [(0, z)]) for z in (2, 4, 6)]  27.6 us
    pallas_call x2, Pallas kernels, update(): pl.pallas_call(lambda *refs: update_kernel(*refs, again=which == 1), grid...  18.3 us
    ppermute x7, starting transfers between devices, exchange(): lax.ppermute(pieces[q], 'row', [(0, 2 * q), (1, 2 * q + 1)])  15.6 us
    ppermute x7, starting transfers between devices, exchange(): parts = [lax.ppermute(strips[z], 'col', [(0, z)]) for z in range(1, COLS)]  14.8 us
    ppermute x8, starting transfers between devices, gather_plane(): return (own, [lax.ppermute(part, 'row', CORE) for part in own])  13.2 us
    pallas_call x1, Pallas kernels, compute(): pl.pallas_call(factor_kernel, grid_spec=pltpu.PrefetchScalarGridSpec(num_...  12.5 us
    ppermute x3, starting transfers between devices, exchange(): parts = [lax.ppermute(core_piece, 'col', [(0, z)]) for z in (2, 4, 6)]  9.24 us
    ppermute x2, starting transfers between devices, gather_plane(): far_odd = lax.ppermute(after[height:], 'row', X_DOWN)  5.44 us
  transfers between devices with their start and end apart: 39, of which 9 were waited for; matrix products, arithmetic and copies ran while one was open for 3% of the time, Pallas kernels for 15%

commit v1 on v0

--- a/solution.py
+++ b/solution.py
@@ -141,39 +141,39 @@
 
 def update_kernel(info, front, kept, *refs, again):
     own, other, lower = refs[:4], refs[4:8], refs[8]
+    step = pl.program_id(0)
     if again:
-        left, _, out, quarter, band, block, sems = refs[9:]
+        left, _, out, quarter, band = refs[9:]
     else:
-        upper, panel, out, quarter, left, band, block, sems = refs[9:]
-        left_of(info, panel, upper, left)
+        upper, panel, out, quarter, left, band = refs[9:]
+
+        @pl.when(step == 0)
+        def _():
+            left_of(info, panel, upper, left)
+
     half = info[8] if again else info[7]
     width = band.shape[1]
-    columns = pl.ds(pl.multiple_of(half * 512, 512), 512)
+    columns = pl.ds(pl.multiple_of(half * 512 + step * width, width), width)
     place_rows(band, own, other, info, columns)
     keep = lax.broadcasted_iota(jnp.int32, (SN, width), 0)
     r = [split(jnp.where(keep < info[4 + s], band[SN * s:SN * s + SN, :], 0.0)) for s in range(NSN)]
     s0 = split(dot3(lower[0], r[0]))
     s1 = split(dot3(lower[1], r[0]) + dot3(lower[2], r[1]))
     s2 = split(dot3(lower[3], r[0]) + dot3(lower[4], r[1]) + dot3(lower[5], r[2]))
-    order = order_of(info, info[2] * 1024 + half * 512, 1, (1, width))
+    order = order_of(info, info[2] * 1024 + half * 512 + step * width, 1, (1, width))
     total = None
     for s, value in enumerate((s0, s1, s2)):
         live = order > s
         masked = tuple(jnp.where(live, part, jnp.zeros_like(part)) for part in value)
         term = dot3(left[:, SN * s:SN * s + SN], masked)
         total = term if total is None else total + term
-    copies = []
     for i in range(4):
         rows = slice(128 * i, 128 * i + 128)
-        result = front[rows, columns] * kept[i:i + 1, columns] - total[rows]
-        block[rows, :] = result
-        copies.append(pltpu.make_async_copy(block.at[rows, :], out.at[rows, columns], sems.at[i]))
-        copies[i].start()
+        result = front[rows, :] * kept[i:i + 1, columns] - total[rows]
+        out[rows, :] = result
         if i % 2:
-            for j in range(2):
+            for j in range(width // 256):
                 quarter[64 * (i - 1):64 * (i + 1), 128 * j:128 * j + 128] = result[:, 256 * j + 128:256 * j + 256]
-    for copy in copies:
-        copy.wait()
 
 
 VMEM_WHOLE = pl.BlockSpec(memory_space=pltpu.VMEM)
@@ -247,23 +247,25 @@
         out_shape=[stacked(6), stacked(3)],
         name="factor",
     )(info, *pivot[0], *pivot[1])
+    width = 512
 
     def update(which, *inputs):
+        def at(j, info):
+            return (0, info[7 + which] * (512 // width) + j)
+
         left_shape = (1024, PIV)
-        anywhere = pl.BlockSpec(memory_space=pl.ANY)
-        specs = [VMEM_WHOLE, anywhere] if which else [VMEM_WHOLE] * len(inputs)
+        specs = [VMEM_WHOLE, pl.BlockSpec(memory_space=pl.ANY)] if which else [VMEM_WHOLE] * len(inputs)
         return pl.pallas_call(
             lambda *refs: update_kernel(*refs, again=which == 1),
             grid_spec=pltpu.PrefetchScalarGridSpec(
                 num_scalar_prefetch=1,
-                grid=(),
-                in_specs=[VMEM_WHOLE] * 11 + specs,
-                out_specs=[anywhere, VMEM_WHOLE] + [VMEM_WHOLE] * (1 - which),
-                scratch_shapes=[
-                    pltpu.VMEM((PIV, 512), jnp.float32),
-                    pltpu.VMEM((512, 512), jnp.float32),
-                    pltpu.SemaphoreType.DMA((4,)),
-                ],
+                grid=(512 // width,),
+                in_specs=[pl.BlockSpec((512, width), at)] + [VMEM_WHOLE] * 10 + specs,
+                out_specs=[
+                    pl.BlockSpec((512, width), at),
+                    pl.BlockSpec((256, width // 2), lambda j, info: (0, j)),
+                ] + [VMEM_WHOLE] * (1 - which),
+                scratch_shapes=[pltpu.VMEM((PIV, width), jnp.float32)],
             ),
             out_shape=[
                 jax.ShapeDtypeStruct((512, 1024), jnp.float32),

time: 159 us -> 157 us (0.987)
  Pallas kernels: 34.3 us -> 32.7 us
    pallas_call x2, Pallas kernels: 18.3 us -> 16.6 us  [update(): pl.pallas_call(lambda *refs: update_kernel(*refs, again=which == 1), grid...]
where the time goes in v1:
time: 157 us
  starting transfers between devices  71.1 us (45%)
  waiting for transfers between devices  40.5 us (26%)
  Pallas kernels  32.7 us (21%)
  other arithmetic  6.4 us (4%)
  local copies, waits for them, and re-layouts  4.58 us (3%)
    ppermute x3, waiting for transfers between devices, exchange(): parts = [lax.ppermute(core_piece, 'col', [(0, z)]) for z in (2, 4, 6)]  27.6 us
    pallas_call x2, Pallas kernels, update(): pl.pallas_call(lambda *refs: update_kernel(*refs, again=which == 1), grid...  16.6 us
    ppermute x7, starting transfers between devices, exchange(): lax.ppermute(pieces[q], 'row', [(0, 2 * q), (1, 2 * q + 1)])  15.6 us
    ppermute x7, starting transfers between devices, exchange(): parts = [lax.ppermute(strips[z], 'col', [(0, z)]) for z in range(1, COLS)]  14.8 us
    ppermute x8, starting transfers between devices, gather_plane(): return (own, [lax.ppermute(part, 'row', CORE) for part in own])  13.2 us
    pallas_call x1, Pallas kernels, compute(): pl.pallas_call(factor_kernel, grid_spec=pltpu.PrefetchScalarGridSpec(num_...  12.5 us
    ppermute x3, starting transfers between devices, exchange(): parts = [lax.ppermute(core_piece, 'col', [(0, z)]) for z in (2, 4, 6)]  9.24 us
    ppermute x2, starting transfers between devices, gather_plane(): far_odd = lax.ppermute(after[height:], 'row', X_DOWN)  5.44 us
  transfers between devices with their start and end apart: 39, of which 9 were waited for; matrix products, arithmetic and copies ran while one was open for 3% of the time, Pallas kernels for 15%

profile of v1, /device:TPU:1, one launch (start us, length us, event | category | flops | bytes accessed | tf_op | source)
XLA Modules:
  0.0 156.7 jit_solution(14860550187998501373)
XLA Ops:
  4.1 1.5 slice_multiply_fusion.5
  5.6 5.7 %collective-permute-start.31 = (f32[64,768]{1,0:T(8,128)S(1)}, f32[64,768]{1,0:T(8,128)S(1)}, u32[]{:S(2)}, u32[]{:S(2)}) collective-permute-start(f32[64,768]{1,0:T(8,128)S(1)} %get-tuple-element.38), channel_id=1, source_target_pairs={{0,4},{1,5},{16,20},{17,21},{32,36},{33,37},{48,52},{49,53},{64,68... | collective-permute-start | bytes 589832 | tf_op jit(solution)/shard_map/ppermute | solution.py:229
  11.4 2.0 %collective-permute-start.32 = (f32[64,768]{1,0:T(8,128)S(1)}, f32[64,768]{1,0:T(8,128)S(1)}, u32[]{:S(2)}, u32[]{:S(2)}) collective-permute-start(f32[64,768]{1,0:T(8,128)S(1)} %get-tuple-element.39), channel_id=1, source_target_pairs={{0,6},{1,7},{16,22},{17,23},{32,38},{33,39},{48,54},{49,55},{64,70... | collective-permute-start | bytes 589832 | tf_op jit(solution)/shard_map/ppermute | solution.py:229
  13.4 1.9 %collective-permute-start.36 = (f32[64,768]{1,0:T(8,128)S(1)}, f32[64,768]{1,0:T(8,128)S(1)}, u32[]{:S(2)}, u32[]{:S(2)}) collective-permute-start(f32[64,768]{1,0:T(8,128)S(1)} %get-tuple-element.44), channel_id=1, source_target_pairs={{0,14},{1,15},{16,30},{17,31},{32,46},{33,47},{48,62},{49,63},{64,... | collective-permute-start | bytes 589832 | tf_op jit(solution)/shard_map/ppermute | solution.py:229
  15.3 1.3 collective-permute-start.35
  18.7 3.5 %pieces.1 = (f32[48,1024]{1,0:T(8,128)}, f32[48,1024]{1,0:T(8,128)}, f32[48,1024]{1,0:T(8,128)}, f32[48,1024]{1,0:T(8,128)}, f32[48,1024]{1,0:T(8,128)}, /*index...) custom-call(s32[9]{0:T(128)} %concatenate.15.info.refs_0_, f32[512,1024]{1,0:T(8,128)} %bitcast.28, ...), custom_call_target="tpu_custom_call" | custom-call | tf_op jit(solution)/shard_map/pieces/pallas_call | solution.py:209
  23.5 1.3 collective-permute-start.30
  24.8 4.2 %collective-permute-start.1 = (f32[48,1024]{1,0:T(8,128)}, f32[48,1024]{1,0:T(8,128)S(1)}, u32[]{:S(2)}, u32[]{:S(2)}) collective-permute-start(f32[48,1024]{1,0:T(8,128)} %get-tuple-element.18), channel_id=1, source_target_pairs={{0,32},{16,48},{1,33},{17,49},{2,34},{18,50},{3,35},{19,51},{4,36}... | collective-permute-start | bytes 589832 | tf_op jit(solution)/shard_map/ppermute | solution.py:220
  29.1 1.3 collective-permute-start.2
  30.4 2.0 %collective-permute-start.3 = (f32[48,1024]{1,0:T(8,128)}, f32[48,1024]{1,0:T(8,128)S(1)}, u32[]{:S(2)}, u32[]{:S(2)}) collective-permute-start(f32[48,1024]{1,0:T(8,128)} %get-tuple-element.20), channel_id=1, source_target_pairs={{0,96},{16,112},{1,97},{17,113},{2,98},{18,114},{3,99},{19,115},{4... | collective-permute-start | bytes 589832 | tf_op jit(solution)/shard_map/ppermute | solution.py:220
  32.5 1.3 collective-permute-start.4
  33.8 4.2 %collective-permute-start.5 = (f32[48,1024]{1,0:T(8,128)}, f32[48,1024]{1,0:T(8,128)S(1)}, u32[]{:S(2)}, u32[]{:S(2)}) collective-permute-start(f32[48,1024]{1,0:T(8,128)} %get-tuple-element.22), channel_id=1, source_target_pairs={{0,160},{16,176},{1,161},{17,177},{2,162},{18,178},{3,163},{19,179... | collective-permute-start | bytes 589832 | tf_op jit(solution)/shard_map/ppermute | solution.py:220
  39.3 1.3 collective-permute-start.7
  42.9 3.9 %all-to-all-start = ((f32[8,64,768]{2,1,0:T(8,128)}), f32[8,64,768]{2,1,0:T(8,128)S(1)}, u32[]{:S(2)}, u32[]{:S(2)}) async-start(f32[8,64,768]{2,1,0:T(8,128)} %broadcast_in_dim.24), calls=%async_computation | async-start | bytes 3145728 | tf_op jit(solution)/shard_map/all_to_all | solution.py:231
  47.0 5.5 %collective-permute-start.19 = (f32[48,768]{1,0:T(8,128)S(1)}, f32[48,768]{1,0:T(8,128)S(1)}, u32[]{:S(2)}, u32[]{:S(2)}) collective-permute-start(f32[48,768]{1,0:T(8,128)S(1)} %slice.97), channel_id=1, source_target_pairs={{0,12},{1,13},{16,28},{17,29},{32,44},{33,45},{48,60},{49,61},{64,... | collective-permute-start | bytes 442376 | tf_op jit(solution)/shard_map/ppermute | solution.py:224
  52.4 2.5 %collective-permute-start.18 = (f32[48,768]{1,0:T(8,128)S(1)}, f32[48,768]{1,0:T(8,128)S(1)}, u32[]{:S(2)}, u32[]{:S(2)}) collective-permute-start(f32[48,768]{1,0:T(8,128)S(1)} %slice.97), channel_id=1, source_target_pairs={{0,8},{1,9},{16,24},{17,25},{32,40},{33,41},{48,56},{49,57},{64,72... | collective-permute-start | bytes 442376 | tf_op jit(solution)/shard_map/ppermute | solution.py:224
  56.2 14.2 %collective-permute-done.19 = f32[48,768]{1,0:T(8,128)S(1)} collective-permute-done((f32[48,768]{1,0:T(8,128)S(1)}, f32[48,768]{1,0:T(8,128)S(1)}, u32[]{:S(2)}, u32[]{:S(2)}) %collective-permute-start.19) | collective-permute-done | bytes 147488 | tf_op jit(solution)/shard_map/ppermute | solution.py:224
  70.4 9.4 %collective-permute-done.18 = f32[48,768]{1,0:T(8,128)S(1)} collective-permute-done((f32[48,768]{1,0:T(8,128)S(1)}, f32[48,768]{1,0:T(8,128)S(1)}, u32[]{:S(2)}, u32[]{:S(2)}) %collective-permute-start.18) | collective-permute-done | bytes 147488 | tf_op jit(solution)/shard_map/ppermute | solution.py:224
  79.8 4.0 %collective-permute-done.17 = f32[48,768]{1,0:T(8,128)S(1)} collective-permute-done((f32[48,768]{1,0:T(8,128)S(1)}, f32[48,768]{1,0:T(8,128)S(1)}, u32[]{:S(2)}, u32[]{:S(2)}) %collective-permute-start.17) | collective-permute-done | bytes 147488 | tf_op jit(solution)/shard_map/ppermute | solution.py:224
  85.3 3.9 %collective-permute-done.20 = f32[48,768]{1,0:T(8,128)S(1)} collective-permute-done((f32[48,768]{1,0:T(8,128)S(1)}, f32[48,768]{1,0:T(8,128)S(1)}, u32[]{:S(2)}, u32[]{:S(2)}) %collective-permute-start.20) | collective-permute-done | bytes 147488 | tf_op jit(solution)/shard_map/ppermute | solution.py:226
  89.4 1.9 %collective-permute-done.8 = f32[48,1024]{1,0:T(8,128)S(1)} collective-permute-done((f32[48,1024]{1,0:T(8,128)S(1)}, f32[48,1024]{1,0:T(8,128)S(1)}, u32[]{:S(2)}, u32[]{:S(2)}) %collective-permute-start.8) | collective-permute-done | bytes 196640 | tf_op jit(solution)/shard_map/ppermute | solution.py:195
  91.5 2.7 %collective-permute-start.9 = (f32[96,1024]{1,0:T(8,128)S(1)}, f32[96,1024]{1,0:T(8,128)S(1)}, u32[]{:S(2)}, u32[]{:S(2)}) collective-permute-start(f32[96,1024]{1,0:T(8,128)S(1)} %pad_maximum_fusion.refs_3_), channel_id=1, source_target_pairs={{0,192},{16,208},{32,224},{48,240},{64,0},{80,16},{96,32},{112,48}... | collective-permute-start | bytes 1179656 | tf_op jit(solution)/shard_map/ppermute | solution.py:198
  95.0 2.7 %collective-permute-start.22 = (f32[96,768]{1,0:T(8,128)S(1)}, f32[96,768]{1,0:T(8,128)S(1)}, u32[]{:S(2)}, u32[]{:S(2)}) collective-permute-start(f32[96,768]{1,0:T(8,128)S(1)} %pad_maximum_fusion.1.refs_0_), channel_id=1, source_target_pairs={{0,192},{16,208},{32,224},{48,240},{64,0},{80,16},{96,32},{112,48}... | collective-permute-start | bytes 884744 | tf_op jit(solution)/shard_map/ppermute | solution.py:198
  97.7 1.9 %collective-permute-done.10.refs_6_ = f32[96,1024]{1,0:T(8,128)S(1)} collective-permute-done((f32[96,1024]{1,0:T(8,128)S(1)}, f32[96,1024]{1,0:T(8,128)S(1)}, u32[]{:S(2)}, u32[]{:S(2)}) %collective-permute-start.10) | collective-permute-done | bytes 393248 | tf_op jit(solution)/shard_map/ppermute | solution.py:197
  99.8 2.7 %collective-permute-start.12 = (f32[48,1024]{1,0:T(8,128)S(1)}, f32[48,1024]{1,0:T(8,128)S(1)}, u32[]{:S(2)}, u32[]{:S(2)}) collective-permute-start(f32[48,1024]{1,0:T(8,128)S(1)} %slice.96), channel_id=1, source_target_pairs={{0,192},{16,208},{32,224},{48,240},{64,0},{80,16},{96,32},{112,48}... | collective-permute-start | bytes 589832 | tf_op jit(solution)/shard_map/ppermute | solution.py:200
  102.5 10.4 %collective-permute-start.26 = (f32[96,768]{1,0:T(8,128)S(1)}, f32[96,768]{1,0:T(8,128)S(1)}, u32[]{:S(2)}, u32[]{:S(2)}) collective-permute-start(f32[96,768]{1,0:T(8,128)S(1)} %pad_maximum_fusion.1.refs_0_), channel_id=1, source_target_pairs={{0,16},{16,0},{32,48},{48,32},{64,80},{80,64},{96,112},{112,96},{1... | collective-permute-start | bytes 884744 | tf_op jit(solution)/shard_map/ppermute | solution.py:202
  113.1 2.7 %collective-permute-start.25 = (f32[48,768]{1,0:T(8,128)S(1)}, f32[48,768]{1,0:T(8,128)S(1)}, u32[]{:S(2)}, u32[]{:S(2)}) collective-permute-start(f32[48,768]{1,0:T(8,128)S(1)} %slice.99), channel_id=1, source_target_pairs={{0,192},{16,208},{32,224},{48,240},{64,0},{80,16},{96,32},{112,48}... | collective-permute-start | bytes 442376 | tf_op jit(solution)/shard_map/ppermute | solution.py:200
  116.6 3.0 %collective-permute-done.24 = f32[48,768]{1,0:T(8,128)S(1)} collective-permute-done((f32[48,768]{1,0:T(8,128)S(1)}, f32[48,768]{1,0:T(8,128)S(1)}, u32[]{:S(2)}, u32[]{:S(2)}) %collective-permute-start.24) | collective-permute-done | bytes 147488 | tf_op jit(solution)/shard_map/ppermute | solution.py:199
  124.1 12.5 %factor.1 = (bf16[6,512,256]{2,1,0:T(8,128)(2,1)}, bf16[3,512,256]{2,1,0:T(8,128)(2,1)}) custom-call(s32[9]{0:T(128)} %concatenate.15.info.refs_0_, f32[96,768]{1,0:T(8,128)} %copy-done.6, f32[96,768]{1,0:T(8,128)} %copy-done.8, f32[96,768]{1,0:T(8,128)} %copy-done.9, f32[96,768]{1,0:T(8,128)} %copy-done.7, f32[96,768]{1,0:T(8,128)} %copy-done.12, ...), custom_call_target="tpu_custom_call" | custom-call | tf_op jit(solution)/shard_map/factor/pallas_call | solution.py:238
  137.9 9.0 %update.2 = (f32[512,1024]{1,0:T(8,128)}, f32[256,256]{1,0:T(8,128)}, bf16[1024,768]{1,0:T(8,128)(2,1)}) custom-call(s32[9]{0:T(128)} %concatenate.15.info.refs_0_, f32[512,1024]{1,0:T(8,128)} %bitcast.30, f32[4,1024]{1,0:T(4,128)} %bitcast.36, f32[96,1024]{1,0:T(8,128)} %copy-done.1, f32[96,1024]{1,0:T(8,128)} %copy-done.3, f32[96,1024]{1,0:T(8,128)} %copy-done.4, ...), custom_call_target="tpu_custom_call" | custom-call | tf_op jit(solution)/shard_map/update/pallas_call | solution.py:258
  147.4 7.6 %update.3 = (f32[512,1024]{1,0:T(8,128)}, f32[256,256]{1,0:T(8,128)}) custom-call(s32[9]{0:T(128)} %concatenate.15.info.refs_0_, f32[512,1024]{1,0:T(8,128)} %bitcast.31, f32[4,1024]{1,0:T(4,128)} %bitcast.37, f32[96,1024]{1,0:T(8,128)} %copy-done.1, f32[96,1024]{1,0:T(8,128)} %copy-done.3, f32[96,1024]{1,0:T(8,128)} %copy-done.4, ...), custom_call_target="tpu_custom_call", output_to_operand_aliasing={{0}: (13, {})} | custom-call | tf_op jit(solution)/shard_map/update/pallas_call | solution.py:258
  155.0 1.7 %add.98 = f32[256,256]{1,0:T(8,128)} add(f32[256,256]{1,0:T(8,128)} %get-tuple-element.30, f32[256,256]{1,0:T(8,128)S(1)} %collective-permute-done.37) | non-fusion elementwise | flops 65536 | bytes 786432 | tf_op jit(solution)/shard_map/add | solution.py:281
  (115 shorter events, 21.3 us)
Async XLA Ops:
  2.6 14.7 %collective-permute-start = (f32[128,1024]{1,0:T(8,128)S(1)}, f32[128,1024]{1,0:T(8,128)S(1)}, u32[]{:S(2)}, u32[]{:S(2)}) collective-permute-start(f32[128,1024]{1,0:T(8,128)S(1)} %bitcast_multiply_fusion), channel_id=1, source_target_pairs={{0,16},{1,17},{2,18},{3,19},{4,20},{5,21},{6,22},{7,23},{8,24},{9,... | collective-permute-start | bytes 1572872 | tf_op jit(solution)/shard_map/ppermute | solution.py:208
  5.6 16.6 %collective-permute-start.31 = (f32[64,768]{1,0:T(8,128)S(1)}, f32[64,768]{1,0:T(8,128)S(1)}, u32[]{:S(2)}, u32[]{:S(2)}) collective-permute-start(f32[64,768]{1,0:T(8,128)S(1)} %get-tuple-element.38), channel_id=1, source_target_pairs={{0,4},{1,5},{16,20},{17,21},{32,36},{33,37},{48,52},{49,53},{64,68... | collective-permute-start | bytes 589832 | tf_op jit(solution)/shard_map/ppermute | solution.py:229
  11.4 12.1 %collective-permute-start.32 = (f32[64,768]{1,0:T(8,128)S(1)}, f32[64,768]{1,0:T(8,128)S(1)}, u32[]{:S(2)}, u32[]{:S(2)}) collective-permute-start(f32[64,768]{1,0:T(8,128)S(1)} %get-tuple-element.39), channel_id=1, source_target_pairs={{0,6},{1,7},{16,22},{17,23},{32,38},{33,39},{48,54},{49,55},{64,70... | collective-permute-start | bytes 589832 | tf_op jit(solution)/shard_map/ppermute | solution.py:229
  13.4 11.4 %collective-permute-start.36 = (f32[64,768]{1,0:T(8,128)S(1)}, f32[64,768]{1,0:T(8,128)S(1)}, u32[]{:S(2)}, u32[]{:S(2)}) collective-permute-start(f32[64,768]{1,0:T(8,128)S(1)} %get-tuple-element.44), channel_id=1, source_target_pairs={{0,14},{1,15},{16,30},{17,31},{32,46},{33,47},{48,62},{49,63},{64,... | collective-permute-start | bytes 589832 | tf_op jit(solution)/shard_map/ppermute | solution.py:229
  15.3 13.8 %collective-permute-start.35 = (f32[64,768]{1,0:T(8,128)S(1)}, f32[64,768]{1,0:T(8,128)S(1)}, u32[]{:S(2)}, u32[]{:S(2)}) collective-permute-start(f32[64,768]{1,0:T(8,128)S(1)} %get-tuple-element.45), channel_id=1, source_target_pairs={{0,12},{1,13},{16,28},{17,29},{32,44},{33,45},{48,60},{49,61},{64,... | collective-permute-start | bytes 589832 | tf_op jit(solution)/shard_map/ppermute | solution.py:229
  17.3 13.1 %collective-permute-start.34 = (f32[64,768]{1,0:T(8,128)S(1)}, f32[64,768]{1,0:T(8,128)S(1)}, u32[]{:S(2)}, u32[]{:S(2)}) collective-permute-start(f32[64,768]{1,0:T(8,128)S(1)} %get-tuple-element.46), channel_id=1, source_target_pairs={{0,10},{1,11},{16,26},{17,27},{32,42},{33,43},{48,58},{49,59},{64,... | collective-permute-start | bytes 589832 | tf_op jit(solution)/shard_map/ppermute | solution.py:229
  22.2 10.3 %collective-permute-start.33 = (f32[64,768]{1,0:T(8,128)S(1)}, f32[64,768]{1,0:T(8,128)S(1)}, u32[]{:S(2)}, u32[]{:S(2)}) collective-permute-start(f32[64,768]{1,0:T(8,128)S(1)} %get-tuple-element.47), channel_id=1, source_target_pairs={{0,8},{1,9},{16,24},{17,25},{32,40},{33,41},{48,56},{49,57},{64,72... | collective-permute-start | bytes 589832 | tf_op jit(solution)/shard_map/ppermute | solution.py:229
  23.5 10.3 %collective-permute-start.30 = (f32[64,768]{1,0:T(8,128)S(1)}, f32[64,768]{1,0:T(8,128)S(1)}, u32[]{:S(2)}, u32[]{:S(2)}) collective-permute-start(f32[64,768]{1,0:T(8,128)S(1)} %get-tuple-element.48), channel_id=1, source_target_pairs={{0,2},{1,3},{16,18},{17,19},{32,34},{33,35},{48,50},{49,51},{64,66... | collective-permute-start | bytes 589832 | tf_op jit(solution)/shard_map/ppermute | solution.py:229
  24.8 13.1 %collective-permute-start.1 = (f32[48,1024]{1,0:T(8,128)}, f32[48,1024]{1,0:T(8,128)S(1)}, u32[]{:S(2)}, u32[]{:S(2)}) collective-permute-start(f32[48,1024]{1,0:T(8,128)} %get-tuple-element.18), channel_id=1, source_target_pairs={{0,32},{16,48},{1,33},{17,49},{2,34},{18,50},{3,35},{19,51},{4,36}... | collective-permute-start | bytes 589832 | tf_op jit(solution)/shard_map/ppermute | solution.py:220
  29.1 10.2 %collective-permute-start.2 = (f32[48,1024]{1,0:T(8,128)}, f32[48,1024]{1,0:T(8,128)S(1)}, u32[]{:S(2)}, u32[]{:S(2)}) collective-permute-start(f32[48,1024]{1,0:T(8,128)} %get-tuple-element.19), channel_id=1, source_target_pairs={{0,64},{16,80},{1,65},{17,81},{2,66},{18,82},{3,67},{19,83},{4,68}... | collective-permute-start | bytes 589832 | tf_op jit(solution)/shard_map/ppermute | solution.py:220
  30.4 16.4 %collective-permute-start.3 = (f32[48,1024]{1,0:T(8,128)}, f32[48,1024]{1,0:T(8,128)S(1)}, u32[]{:S(2)}, u32[]{:S(2)}) collective-permute-start(f32[48,1024]{1,0:T(8,128)} %get-tuple-element.20), channel_id=1, source_target_pairs={{0,96},{16,112},{1,97},{17,113},{2,98},{18,114},{3,99},{19,115},{4... | collective-permute-start | bytes 589832 | tf_op jit(solution)/shard_map/ppermute | solution.py:220
  32.5 14.3 %collective-permute-start.4 = (f32[48,1024]{1,0:T(8,128)}, f32[48,1024]{1,0:T(8,128)S(1)}, u32[]{:S(2)}, u32[]{:S(2)}) collective-permute-start(f32[48,1024]{1,0:T(8,128)} %get-tuple-element.21), channel_id=1, source_target_pairs={{0,128},{16,144},{1,129},{17,145},{2,130},{18,146},{3,131},{19,147... | collective-permute-start | bytes 589832 | tf_op jit(solution)/shard_map/ppermute | solution.py:220
  33.8 13.0 %collective-permute-start.5 = (f32[48,1024]{1,0:T(8,128)}, f32[48,1024]{1,0:T(8,128)S(1)}, u32[]{:S(2)}, u32[]{:S(2)}) collective-permute-start(f32[48,1024]{1,0:T(8,128)} %get-tuple-element.22), channel_id=1, source_target_pairs={{0,160},{16,176},{1,161},{17,177},{2,162},{18,178},{3,163},{19,179... | collective-permute-start | bytes 589832 | tf_op jit(solution)/shard_map/ppermute | solution.py:220
  38.0 8.9 %collective-permute-start.6 = (f32[48,1024]{1,0:T(8,128)}, f32[48,1024]{1,0:T(8,128)S(1)}, u32[]{:S(2)}, u32[]{:S(2)}) collective-permute-start(f32[48,1024]{1,0:T(8,128)} %get-tuple-element.23), channel_id=1, source_target_pairs={{0,192},{16,208},{1,193},{17,209},{2,194},{18,210},{3,195},{19,211... | collective-permute-start | bytes 589832 | tf_op jit(solution)/shard_map/ppermute | solution.py:220
  39.3 7.5 %collective-permute-start.7 = (f32[48,1024]{1,0:T(8,128)}, f32[48,1024]{1,0:T(8,128)S(1)}, u32[]{:S(2)}, u32[]{:S(2)}) collective-permute-start(f32[48,1024]{1,0:T(8,128)} %get-tuple-element.24), channel_id=1, source_target_pairs={{0,224},{16,240},{1,225},{17,241},{2,226},{18,242},{3,227},{19,243... | collective-permute-start | bytes 589832 | tf_op jit(solution)/shard_map/ppermute | solution.py:220
  42.9 93.8 %all-to-all-start = ((f32[8,64,768]{2,1,0:T(8,128)}), f32[8,64,768]{2,1,0:T(8,128)S(1)}, u32[]{:S(2)}, u32[]{:S(2)}) async-start(f32[8,64,768]{2,1,0:T(8,128)} %broadcast_in_dim.24), calls=%async_computation | async-start | bytes 3145728 | tf_op jit(solution)/shard_map/all_to_all | solution.py:231
  47.0 23.5 %collective-permute-start.19 = (f32[48,768]{1,0:T(8,128)S(1)}, f32[48,768]{1,0:T(8,128)S(1)}, u32[]{:S(2)}, u32[]{:S(2)}) collective-permute-start(f32[48,768]{1,0:T(8,128)S(1)} %slice.97), channel_id=1, source_target_pairs={{0,12},{1,13},{16,28},{17,29},{32,44},{33,45},{48,60},{49,61},{64,... | collective-permute-start | bytes 442376 | tf_op jit(solution)/shard_map/ppermute | solution.py:224
  52.4 27.3 %collective-permute-start.18 = (f32[48,768]{1,0:T(8,128)S(1)}, f32[48,768]{1,0:T(8,128)S(1)}, u32[]{:S(2)}, u32[]{:S(2)}) collective-permute-start(f32[48,768]{1,0:T(8,128)S(1)} %slice.97), channel_id=1, source_target_pairs={{0,8},{1,9},{16,24},{17,25},{32,40},{33,41},{48,56},{49,57},{64,72... | collective-permute-start | bytes 442376 | tf_op jit(solution)/shard_map/ppermute | solution.py:224
  54.9 28.9 %collective-permute-start.17 = (f32[48,768]{1,0:T(8,128)S(1)}, f32[48,768]{1,0:T(8,128)S(1)}, u32[]{:S(2)}, u32[]{:S(2)}) collective-permute-start(f32[48,768]{1,0:T(8,128)S(1)} %slice.97), channel_id=1, source_target_pairs={{0,4},{1,5},{16,20},{17,21},{32,36},{33,37},{48,52},{49,53},{64,68... | collective-permute-start | bytes 442376 | tf_op jit(solution)/shard_map/ppermute | solution.py:224
  91.4 8.2 %collective-permute-start.10 = (f32[96,1024]{1,0:T(8,128)S(1)}, f32[96,1024]{1,0:T(8,128)S(1)}, u32[]{:S(2)}, u32[]{:S(2)}) collective-permute-start(f32[96,1024]{1,0:T(8,128)S(1)} %pad_maximum_fusion.refs_3_), channel_id=1, source_target_pairs={{0,64},{16,80},{32,96},{48,112},{64,128},{80,144},{96,160},{112,17... | collective-permute-start | bytes 1179656 | tf_op jit(solution)/shard_map/ppermute | solution.py:197
  91.5 8.2 %collective-permute-start.9 = (f32[96,1024]{1,0:T(8,128)S(1)}, f32[96,1024]{1,0:T(8,128)S(1)}, u32[]{:S(2)}, u32[]{:S(2)}) collective-permute-start(f32[96,1024]{1,0:T(8,128)S(1)} %pad_maximum_fusion.refs_3_), channel_id=1, source_target_pairs={{0,192},{16,208},{32,224},{48,240},{64,0},{80,16},{96,32},{112,48}... | collective-permute-start | bytes 1179656 | tf_op jit(solution)/shard_map/ppermute | solution.py:198
  94.9 18.0 %collective-permute-start.23 = (f32[96,768]{1,0:T(8,128)S(1)}, f32[96,768]{1,0:T(8,128)S(1)}, u32[]{:S(2)}, u32[]{:S(2)}) collective-permute-start(f32[96,768]{1,0:T(8,128)S(1)} %pad_maximum_fusion.1.refs_0_), channel_id=1, source_target_pairs={{0,64},{16,80},{32,96},{48,112},{64,128},{80,144},{96,160},{112,17... | collective-permute-start | bytes 884744 | tf_op jit(solution)/shard_map/ppermute | solution.py:197
  95.0 18.0 %collective-permute-start.22 = (f32[96,768]{1,0:T(8,128)S(1)}, f32[96,768]{1,0:T(8,128)S(1)}, u32[]{:S(2)}, u32[]{:S(2)}) collective-permute-start(f32[96,768]{1,0:T(8,128)S(1)} %pad_maximum_fusion.1.refs_0_), channel_id=1, source_target_pairs={{0,192},{16,208},{32,224},{48,240},{64,0},{80,16},{96,32},{112,48}... | collective-permute-start | bytes 884744 | tf_op jit(solution)/shard_map/ppermute | solution.py:198
  99.6 16.2 %collective-permute-start.11 = (f32[48,1024]{1,0:T(8,128)S(1)}, f32[48,1024]{1,0:T(8,128)S(1)}, u32[]{:S(2)}, u32[]{:S(2)}) collective-permute-start(f32[48,1024]{1,0:T(8,128)S(1)} %slice.95), channel_id=1, source_target_pairs={{0,64},{16,80},{32,96},{48,112},{64,128},{80,144},{96,160},{112,17... | collective-permute-start | bytes 589832 | tf_op jit(solution)/shard_map/ppermute | solution.py:199
  99.8 16.7 %collective-permute-start.12 = (f32[48,1024]{1,0:T(8,128)S(1)}, f32[48,1024]{1,0:T(8,128)S(1)}, u32[]{:S(2)}, u32[]{:S(2)}) collective-permute-start(f32[48,1024]{1,0:T(8,128)S(1)} %slice.96), channel_id=1, source_target_pairs={{0,192},{16,208},{32,224},{48,240},{64,0},{80,16},{96,32},{112,48}... | collective-permute-start | bytes 589832 | tf_op jit(solution)/shard_map/ppermute | solution.py:200
  102.5 18.0 %collective-permute-start.26 = (f32[96,768]{1,0:T(8,128)S(1)}, f32[96,768]{1,0:T(8,128)S(1)}, u32[]{:S(2)}, u32[]{:S(2)}) collective-permute-start(f32[96,768]{1,0:T(8,128)S(1)} %pad_maximum_fusion.1.refs_0_), channel_id=1, source_target_pairs={{0,16},{16,0},{32,48},{48,32},{64,80},{80,64},{96,112},{112,96},{1... | collective-permute-start | bytes 884744 | tf_op jit(solution)/shard_map/ppermute | solution.py:202
  113.1 7.6 %collective-permute-start.25 = (f32[48,768]{1,0:T(8,128)S(1)}, f32[48,768]{1,0:T(8,128)S(1)}, u32[]{:S(2)}, u32[]{:S(2)}) collective-permute-start(f32[48,768]{1,0:T(8,128)S(1)} %slice.99), channel_id=1, source_target_pairs={{0,192},{16,208},{32,224},{48,240},{64,0},{80,16},{96,32},{112,48}... | collective-permute-start | bytes 442376 | tf_op jit(solution)/shard_map/ppermute | solution.py:200
  119.6 17.0 %collective-permute-start.13 = (f32[96,1024]{1,0:T(8,128)S(1)}, f32[96,1024]{1,0:T(8,128)S(1)}, u32[]{:S(2)}, u32[]{:S(2)}) collective-permute-start(f32[96,1024]{1,0:T(8,128)S(1)} %pad_maximum_fusion.refs_3_), channel_id=1, source_target_pairs={{0,16},{16,0},{32,48},{48,32},{64,80},{80,64},{96,112},{112,96},{1... | collective-permute-start | bytes 1179656 | tf_op jit(solution)/shard_map/ppermute | solution.py:202
  120.5 16.1 %collective-permute-start.16 = (f32[96,1024]{1,0:T(8,128)S(1)}, f32[96,1024]{1,0:T(8,128)}, u32[]{:S(2)}, u32[]{:S(2)}) collective-permute-start(f32[96,1024]{1,0:T(8,128)S(1)} %collective-permute-done.10.refs_6_), channel_id=1, source_target_pairs={{0,16},{16,0},{32,48},{48,32},{64,80},{80,64},{96,112},{112,96},{1... | collective-permute-start | bytes 1179656 | tf_op jit(solution)/shard_map/ppermute | solution.py:202
  120.6 16.0 %collective-permute-start.14 = (f32[96,1024]{1,0:T(8,128)S(1)}, f32[96,1024]{1,0:T(8,128)}, u32[]{:S(2)}, u32[]{:S(2)}) collective-permute-start(f32[96,1024]{1,0:T(8,128)S(1)} %collective-permute-done.9.refs_4_), channel_id=1, source_target_pairs={{0,16},{16,0},{32,48},{48,32},{64,80},{80,64},{96,112},{112,96},{1... | collective-permute-start | bytes 1179656 | tf_op jit(solution)/shard_map/ppermute | solution.py:202
  121.1 15.5 %collective-permute-start.15 = (f32[96,1024]{1,0:T(8,128)S(1)}, f32[96,1024]{1,0:T(8,128)}, u32[]{:S(2)}, u32[]{:S(2)}) collective-permute-start(f32[96,1024]{1,0:T(8,128)S(1)} %constant_dynamic-update-slice_fusion.refs_5_), channel_id=1, source_target_pairs={{0,16},{16,0},{32,48},{48,32},{64,80},{80,64},{96,112},{112,96},{1... | collective-permute-start | bytes 1179656 | tf_op jit(solution)/shard_map/ppermute | solution.py:202
  147.0 8.0 %collective-permute-start.37 = (f32[256,256]{1,0:T(8,128)}, f32[256,256]{1,0:T(8,128)S(1)}, u32[]{:S(2)}, u32[]{:S(2)}) collective-permute-start(f32[256,256]{1,0:T(8,128)} %get-tuple-element.31), channel_id=1, source_target_pairs={{0,1},{1,0},{2,3},{3,2},{4,5},{5,4},{6,7},{7,6},{8,9},{9,8},{10,11... | collective-permute-start | bytes 786440 | tf_op jit(solution)/shard_map/ppermute | solution.py:279
  (24 other events, 261.8 us)
